TPU v7x, 256 devices: a whole 4x4x8 slice. The times are simulated.
256 devices in a mesh: seq: 32 (over z, y), head: 8 (over x, core).
Axes of the slice: x: 4, y: 4, z: 8, core: 2. Of those that a mesh axis runs over, the one named last changes fastest.
Arguments:
- query_in: bfloat16 [32768, 32, 128], P(('seq', 'head')), may hold values from -6 to 6
- key_in: bfloat16 [32768, 32, 128], P(('seq', 'head')), may hold values from -6 to 6
- value_in: bfloat16 [32768, 32, 128], P(('seq', 'head')), may hold values from -6 to 6
- grad_out: bfloat16 [32768, 32, 128], P(('seq', 'head')), may hold values from -6 to 6
- log_decay: bfloat16 [32768, 32], P(('seq', 'head')), may hold values from -1 to 0, as said below
Outputs:
- attended: bfloat16 [32768, 32, 128], P(('seq', 'head'))
- grad_query: bfloat16 [32768, 32, 128], P(('seq', 'head'))
- grad_key: bfloat16 [32768, 32, 128], P(('seq', 'head'))
- grad_value: bfloat16 [32768, 32, 128], P(('seq', 'head'))
Inputs may be any that keep to these rules, and one draw needn't show every extreme that they name: Every entry of log_decay is negative.
All inputs are finite; a program needn't handle non-finite values.
Results may differ from a plain program's by a relative error of at most 0.007.
Values may be sent and summed in bfloat16 or wider, within the bound.
A program may use at most 128 MiB of HBM per device.

v0:
```python
import jax
import jax.numpy as jnp
from jax import lax
from jax.sharding import PartitionSpec as P

precise = lax.Precision.HIGHEST


def shards(query_in, key_in, value_in, grad_out, log_decay):
    f32 = jnp.float32
    bf16 = jnp.bfloat16
    queries, keys_all, values, grads, token_decays = (
        lax.all_to_all(query_in, "head", split_axis=1, concat_axis=0, tiled=True),
        lax.all_to_all(key_in, "head", split_axis=1, concat_axis=0, tiled=True),
        lax.all_to_all(value_in, "head", split_axis=1, concat_axis=0, tiled=True),
        lax.all_to_all(grad_out, "head", split_axis=1, concat_axis=0, tiled=True),
        lax.all_to_all(log_decay, "head", split_axis=1, concat_axis=0, tiled=True),
    )
    segment_length = queries.shape[0]
    width = queries.shape[2]
    scaling = 1.0 / width
    within = jnp.cumsum(token_decays.astype(f32), axis=0)
    seg_total = within[-1]
    to_start = jnp.exp(within)[:, :, None]
    to_end = jnp.exp(seg_total[None, :] - within)[:, :, None]
    keys_end = (keys_all.astype(f32) * to_end).astype(bf16)
    values_end = (values.astype(f32) * to_end).astype(bf16)
    queries_start = (queries.astype(f32) * to_start).astype(bf16)
    grads_start = (grads.astype(f32) * to_start).astype(bf16)
    local_kv = jnp.einsum("thd,the->hde", keys_end, values, preferred_element_type=f32).astype(bf16)
    local_qg = jnp.einsum("thd,the->hde", queries_start, grads, preferred_element_type=f32).astype(
        bf16
    )
    seg_count = lax.axis_size("seq")
    seq_place = lax.axis_index("seq")
    totals = lax.all_gather(seg_total[None, :], "seq", axis=0, tiled=True)
    cum_inc = jnp.cumsum(totals, axis=0)
    cum_exc = cum_inc - totals
    mine_inc = lax.dynamic_index_in_dim(cum_inc, seq_place, 0, keepdims=False)
    mine_exc = lax.dynamic_index_in_dim(cum_exc, seq_place, 0, keepdims=False)
    ranks = jnp.arange(seg_count)[:, None]
    earlier = ranks < seq_place
    later_on = ranks > seq_place
    w_in = jnp.where(earlier, jnp.exp(jnp.where(earlier, mine_exc[None, :] - cum_inc, 0.0)), 0.0)
    w_out = jnp.where(later_on, jnp.exp(jnp.where(later_on, cum_exc - mine_inc[None, :], 0.0)), 0.0)
    new_in = jnp.einsum(
        "ih,ihde->hde",
        w_in,
        lax.all_gather(local_kv[None], "seq", axis=0, tiled=True).astype(f32),
        precision=precise,
    )
    new_out = jnp.einsum(
        "ih,ihde->hde",
        w_out,
        lax.all_gather(local_qg[None], "seq", axis=0, tiled=True).astype(f32),
        precision=precise,
    )
    state_in = new_in
    state_out = new_out
    state_in = state_in.astype(bf16)
    state_out = state_out.astype(bf16)
    head_specific = within.T
    causal = jnp.arange(segment_length)[:, None] >= jnp.arange(segment_length)[None, :]
    decay_mat = jnp.where(
        causal,
        jnp.exp(jnp.where(causal, head_specific[:, :, None] - head_specific[:, None, :], 0.0)),
        0.0,
    )
    scores = jnp.einsum("thd,shd->hts", queries, keys_all, preferred_element_type=f32)
    attn_w = (scaling * scores * decay_mat).astype(bf16)
    intra = jnp.einsum("hts,shd->thd", attn_w, values, preferred_element_type=f32)
    attended = (
        intra
        + scaling * jnp.einsum("thd,hde->the", queries_start, state_in, preferred_element_type=f32)
    ).astype(bf16)
    back_raw = jnp.einsum("the,she->hts", grads, values, preferred_element_type=f32)
    back_w = (scaling * back_raw * decay_mat).astype(bf16)
    grad_query = (
        jnp.einsum("hts,shd->thd", back_w, keys_all, preferred_element_type=f32)
        + scaling * jnp.einsum("the,hde->thd", grads_start, state_in, preferred_element_type=f32)
    ).astype(bf16)
    grad_key = (
        jnp.einsum("hts,thd->shd", back_w, queries, preferred_element_type=f32)
        + scaling * jnp.einsum("she,hde->shd", values_end, state_out, preferred_element_type=f32)
    ).astype(bf16)
    grad_value = (
        jnp.einsum("hts,the->she", attn_w, grads, preferred_element_type=f32)
        + scaling * jnp.einsum("shd,hde->she", keys_end, state_out, preferred_element_type=f32)
    ).astype(bf16)
    results = (
        lax.all_to_all(attended, "head", split_axis=0, concat_axis=1, tiled=True),
        lax.all_to_all(grad_query, "head", split_axis=0, concat_axis=1, tiled=True),
        lax.all_to_all(grad_key, "head", split_axis=0, concat_axis=1, tiled=True),
        lax.all_to_all(grad_value, "head", split_axis=0, concat_axis=1, tiled=True),
    )
    return (results[0], results[1], results[2], results[3])


def solution(mesh):
    return jax.shard_map(
        shards,
        mesh=mesh,
        in_specs=(
            P(("seq", "head"), None, None),
            P(("seq", "head"), None, None),
            P(("seq", "head"), None, None),
            P(("seq", "head"), None, None),
            P(("seq", "head"), None),
        ),
        out_specs=(
            P(("seq", "head"), None, None),
            P(("seq", "head"), None, None),
            P(("seq", "head"), None, None),
            P(("seq", "head"), None, None),
        ),
        check_vma=False,
    )
```

profile of v0, /device:TPU:1, one launch (start us, length us, event | category | flops | bytes accessed | tf_op | source)
XLA Modules:
  0.0 300.9 jit_solution(2192634646455913351)
XLA Ops:
  7.2 6.6 %all-to-all-start.2 = ((bf16[128,8,4]{0,2,1:T(4,128)(2,1)}), bf16[128,8,4]{0,2,1:T(4,128)(2,1)S(1)}, u32[]{:S(2)}, u32[]{:S(2)}) async-start(bf16[128,8,4]{0,2,1:T(4,128)(2,1)} %bitcast.154), calls=%async_computation.2 | async-start | bytes 16384 | tf_op jit(solution)/shard_map/all_to_all | solution.py:17
  13.8 2.6 copy.120
  16.4 2.0 all-to-all-done.2
  18.4 4.2 %all-to-all-start.1 = ((bf16[128,32,128]{2,0,1:T(8,128)(2,1)}), bf16[128,32,128]{2,0,1:T(8,128)(2,1)S(1)}, u32[]{:S(2)}, u32[]{:S(2)}) async-start(bf16[128,32,128]{2,0,1:T(8,128)(2,1)} %copy.120), calls=%async_computation.1 | async-start | bytes 2097152 | tf_op jit(solution)/shard_map/all_to_all | solution.py:14
  23.9 13.6 %all-to-all-done.1 = bf16[128,32,128]{2,0,1:T(8,128)(2,1)S(1)} async-done(((bf16[128,32,128]{2,0,1:T(8,128)(2,1)}), bf16[128,32,128]{2,0,1:T(8,128)(2,1)S(1)}, u32[]{:S(2)}, u32[]{:S(2)}) %all-to-all-start.1) | async-done | bytes 1048608 | tf_op jit(solution)/shard_map/all_to_all | solution.py:14
  37.6 4.4 %all-to-all-start.3 = ((bf16[128,32,128]{2,0,1:T(8,128)(2,1)}), bf16[128,32,128]{2,0,1:T(8,128)(2,1)S(1)}, u32[]{:S(2)}, u32[]{:S(2)}) async-start(bf16[128,32,128]{2,0,1:T(8,128)(2,1)} %copy.122), calls=%async_computation.3 | async-start | bytes 2097152 | tf_op jit(solution)/shard_map/all_to_all | solution.py:15
  44.0 13.0 %all-to-all-done.3 = bf16[128,32,128]{2,0,1:T(8,128)(2,1)S(1)} async-done(((bf16[128,32,128]{2,0,1:T(8,128)(2,1)}), bf16[128,32,128]{2,0,1:T(8,128)(2,1)S(1)}, u32[]{:S(2)}, u32[]{:S(2)}) %all-to-all-start.3) | async-done | bytes 1048608 | tf_op jit(solution)/shard_map/all_to_all | solution.py:15
  60.1 2.6 copy.118
  62.7 4.4 %all-to-all-start = ((bf16[128,32,128]{2,0,1:T(8,128)(2,1)}), bf16[128,32,128]{2,0,1:T(8,128)(2,1)S(1)}, u32[]{:S(2)}, u32[]{:S(2)}) async-start(bf16[128,32,128]{2,0,1:T(8,128)(2,1)} %copy.118), calls=%async_computation | async-start | bytes 2097152 | tf_op jit(solution)/shard_map/all_to_all | solution.py:13
  68.5 13.6 %all-to-all-done = bf16[128,32,128]{2,0,1:T(8,128)(2,1)S(1)} async-done(((bf16[128,32,128]{2,0,1:T(8,128)(2,1)}), bf16[128,32,128]{2,0,1:T(8,128)(2,1)S(1)}, u32[]{:S(2)}, u32[]{:S(2)}) %all-to-all-start) | async-done | bytes 1048608 | tf_op jit(solution)/shard_map/all_to_all | solution.py:13
  82.1 4.4 %all-to-all-start.5 = ((bf16[128,32,128]{2,0,1:T(8,128)(2,1)}), bf16[128,32,128]{2,0,1:T(8,128)(2,1)S(1)}, u32[]{:S(2)}, u32[]{:S(2)}) async-start(bf16[128,32,128]{2,0,1:T(8,128)(2,1)} %copy.132), calls=%async_computation.5 | async-start | bytes 2097152 | tf_op jit(solution)/shard_map/all_to_all | solution.py:16
  86.6 14.9 %all-to-all-done.5 = bf16[128,32,128]{2,0,1:T(8,128)(2,1)S(1)} async-done(((bf16[128,32,128]{2,0,1:T(8,128)(2,1)}), bf16[128,32,128]{2,0,1:T(8,128)(2,1)S(1)}, u32[]{:S(2)}, u32[]{:S(2)}) %all-to-all-start.5) | async-done | bytes 1048608 | tf_op jit(solution)/shard_map/all_to_all | solution.py:16
  101.6 2.0 convolution_convert_fusion
  104.0 38.2 %all-gather.2 = f32[32,1,4]{2,1,0:T(1,128)S(1)} all-gather(f32[1,1,4]{2,1,0:T(1,128)S(1)} %bitcast.155), channel_id=1, replica_groups=mesh['seq'=32,'head'=8] {'seq'}, dimensions={0}, use_global_device_ids=true | all-gather | bytes 528 | tf_op jit(solution)/shard_map/all_gather | solution.py:36
  142.7 7.4 %multiply_convert_fusion = bf16[4,1024,1024]{2,1,0:T(8,128)(2,1)S(1)} fusion(bf16[1024,4,128]{2,0,1:T(8,128)(2,1)S(1)} %bitcast.118, bf16[1024,4,128]{2,0,1:T(8,128)(2,1)} %bitcast.139, f32[4,1024]{1,0:T(4,128)S(1)} %bitcast.150, pred[1024,1024]{1,0:T(8,128)(4,1)S(1)} %iota_compare_fusion), kind=kOutput, calls=%fused_computation | convolution fusion | flops 1098907648 | bytes 11550720 | tf_op jit(solution)/shard_map/the,she->hts/dot_general | solution.py:76
  150.1 4.0 %fusion.14 = f32[4,1024,128]{2,1,0:T(8,128)} fusion(bf16[4,1024,1024]{2,1,0:T(8,128)(2,1)S(1)} %multiply_convert_fusion, bf16[1024,4,128]{2,0,1:T(8,128)(2,1)S(1)} %bitcast.135), kind=kOutput, calls=%fused_computation.43 | convolution fusion | flops 1073741824 | bytes 11534336 | tf_op jit(solution)/shard_map/hts,shd->thd/dot_general | solution.py:79
  154.0 7.8 %multiply_convert_fusion.1 = bf16[4,1024,1024]{2,1,0:T(8,128)(2,1)} fusion(bf16[1024,4,128]{2,0,1:T(8,128)(2,1)S(1)} %bitcast.122, bf16[1024,4,128]{2,0,1:T(8,128)(2,1)S(1)} %bitcast.136, f32[4,1024]{1,0:T(4,128)S(1)} %bitcast.151, pred[1024,1024]{1,0:T(8,128)(4,1)S(1)} %iota_compare_fusion), kind=kOutput, calls=%fused_computation.1 | convolution fusion | flops 1098907648 | bytes 11550720 | tf_op jit(solution)/shard_map/thd,shd->hts/dot_general | solution.py:69
  161.8 5.8 %fusion = f32[4,1,128,128]{3,1,2,0:T(1,128)S(1)} fusion(f32[32,4,1,1]{0,2,3,1:T(1,128)S(1)} %copy.148, bf16[32,4,128,128]{3,2,1,0:T(8,128)(2,1)} %bitcast.125), kind=kOutput, calls=%fused_computation.4 | convolution fusion | flops 25165824 | bytes 4456960 | tf_op jit(solution)/shard_map/ih,ihde->hde/dot_general | solution.py:46
  170.4 8.2 %all-to-all-start.6 = ((bf16[1024,4,128]{2,1,0:T(4,128)(2,1)}), bf16[1024,4,128]{2,1,0:T(4,128)(2,1)S(1)}, u32[]{:S(2)}, u32[]{:S(2)}) async-start(bf16[1024,4,128]{2,1,0:T(4,128)(2,1)} %copy.135), calls=%async_computation.6 | async-start | bytes 2097152 | tf_op jit(solution)/shard_map/all_to_all | solution.py:92
  178.6 7.7 %fusion.15 = f32[4,1024,128]{2,1,0:T(8,128)} fusion(bf16[4,1024,1024]{2,1,0:T(8,128)(2,1)} %copy-done, bf16[1024,4,128]{2,0,1:T(8,128)(2,1)S(1)} %bitcast.123), kind=kOutput, calls=%fused_computation.44 | convolution fusion | flops 1073741824 | bytes 11534336 | tf_op jit(solution)/shard_map/hts,thd->shd/dot_general | solution.py:83
  186.3 34.8 %all-gather.8.cloned.1.call-done = bf16[128,128,128]{2,1,0:T(8,128)(2,1)} async-done(((bf16[4,128,128]{2,1,0:T(8,128)(2,1)}), bf16[128,128,128]{2,1,0:T(8,128)(2,1)}) %all-gather.8.cloned.1.call-update) | async-done | bytes 4194320 | tf_op jit(solution)/shard_map/all_gather | solution.py:55
  221.1 3.7 %multiply_reduce_fusion = bf16[4,128,128]{2,1,0:T(8,128)(2,1)} fusion(bf16[4,32,128,128]{3,2,0,1:T(8,128)(2,1)} %bitcast.126, f32[4,32]{0,1:T(8,128)S(1)} %get-tuple-element.4), kind=kLoop, calls=%fused_computation.3 | loop fusion | flops 6225920 | bytes 4325888
  225.9 2.7 fusion.3
  230.3 8.5 %all-to-all-start.7 = ((bf16[1024,4,128]{2,1,0:T(4,128)(2,1)}), bf16[1024,4,128]{2,1,0:T(4,128)(2,1)}, u32[]{:S(2)}, u32[]{:S(2)}) async-start(bf16[1024,4,128]{2,1,0:T(4,128)(2,1)} %copy.141), calls=%async_computation.7 | async-start | bytes 2097152 | tf_op jit(solution)/shard_map/all_to_all | solution.py:93
  238.8 5.9 %fusion.13 = f32[4,1024,128]{2,1,0:T(8,128)S(1)} fusion(bf16[4,1024,1024]{2,1,0:T(8,128)(2,1)} %multiply_convert_fusion.1, bf16[1024,4,128]{2,0,1:T(8,128)(2,1)} %bitcast.141), kind=kOutput, calls=%fused_computation.42 | convolution fusion | flops 1073741824 | bytes 11534336 | tf_op jit(solution)/shard_map/hts,shd->thd/dot_general | solution.py:71
  247.5 6.3 %all-to-all-done.7 = bf16[1024,4,128]{2,1,0:T(4,128)(2,1)} async-done(((bf16[1024,4,128]{2,1,0:T(4,128)(2,1)}), bf16[1024,4,128]{2,1,0:T(4,128)(2,1)}, u32[]{:S(2)}, u32[]{:S(2)}) %all-to-all-start.7) | async-done | bytes 1048608 | tf_op jit(solution)/shard_map/all_to_all | solution.py:93
  253.8 4.4 %all-to-all-start.4 = ((bf16[1024,4,128]{2,1,0:T(4,128)(2,1)}), bf16[1024,4,128]{2,1,0:T(4,128)(2,1)S(1)}, u32[]{:S(2)}, u32[]{:S(2)}) async-start(bf16[1024,4,128]{2,1,0:T(4,128)(2,1)} %copy.130), calls=%async_computation.4 | async-start | bytes 2097152 | tf_op jit(solution)/shard_map/all_to_all | solution.py:91
  258.3 6.4 %fusion.16 = f32[4,1024,128]{2,1,0:T(8,128)S(1)} fusion(bf16[4,1024,1024]{2,1,0:T(8,128)(2,1)} %multiply_convert_fusion.1, bf16[1024,4,128]{2,0,1:T(8,128)(2,1)S(1)} %bitcast.120), kind=kOutput, calls=%fused_computation.45 | convolution fusion | flops 1073741824 | bytes 11534336 | tf_op jit(solution)/shard_map/hts,the->she/dot_general | solution.py:87
  267.5 5.8 %all-to-all-done.4 = bf16[1024,4,128]{2,1,0:T(4,128)(2,1)S(1)} async-done(((bf16[1024,4,128]{2,1,0:T(4,128)(2,1)}), bf16[1024,4,128]{2,1,0:T(4,128)(2,1)S(1)}, u32[]{:S(2)}, u32[]{:S(2)}) %all-to-all-start.4) | async-done | bytes 1048608 | tf_op jit(solution)/shard_map/all_to_all | solution.py:91
  273.3 4.4 %all-to-all-start.8 = ((bf16[1024,4,128]{2,1,0:T(4,128)(2,1)}), bf16[1024,4,128]{2,1,0:T(4,128)(2,1)S(1)}, u32[]{:S(2)}, u32[]{:S(2)}) async-start(bf16[1024,4,128]{2,1,0:T(4,128)(2,1)} %copy.145), calls=%async_computation.8 | async-start | bytes 2097152 | tf_op jit(solution)/shard_map/all_to_all | solution.py:94
  279.0 2.6 copy.142
  282.9 9.8 %all-to-all-done.8 = bf16[1024,4,128]{2,1,0:T(4,128)(2,1)S(1)} async-done(((bf16[1024,4,128]{2,1,0:T(4,128)(2,1)}), bf16[1024,4,128]{2,1,0:T(4,128)(2,1)S(1)}, u32[]{:S(2)}, u32[]{:S(2)}) %all-to-all-start.8) | async-done | bytes 1048608 | tf_op jit(solution)/shard_map/all_to_all | solution.py:94
  (63 shorter events, 23.9 us)
Async XLA Ops:
  7.2 15.4 %copy-start.6 = (bf16[128,32,128]{2,1,0:T(8,128)(2,1)S(1)}, bf16[128,32,128]{2,1,0:T(8,128)(2,1)}, u32[]{:S(2)}) copy-start(bf16[128,32,128]{2,1,0:T(8,128)(2,1)} %param.7) | copy-start | bytes 3145732
  7.2 11.2 %all-to-all-start.2 = ((bf16[128,8,4]{0,2,1:T(4,128)(2,1)}), bf16[128,8,4]{0,2,1:T(4,128)(2,1)S(1)}, u32[]{:S(2)}, u32[]{:S(2)}) async-start(bf16[128,8,4]{0,2,1:T(4,128)(2,1)} %bitcast.154), calls=%async_computation.2 | async-start | bytes 16384 | tf_op jit(solution)/shard_map/all_to_all | solution.py:17
  18.4 19.2 %all-to-all-start.1 = ((bf16[128,32,128]{2,0,1:T(8,128)(2,1)}), bf16[128,32,128]{2,0,1:T(8,128)(2,1)S(1)}, u32[]{:S(2)}, u32[]{:S(2)}) async-start(bf16[128,32,128]{2,0,1:T(8,128)(2,1)} %copy.120), calls=%async_computation.1 | async-start | bytes 2097152 | tf_op jit(solution)/shard_map/all_to_all | solution.py:14
  37.6 19.4 %all-to-all-start.3 = ((bf16[128,32,128]{2,0,1:T(8,128)(2,1)}), bf16[128,32,128]{2,0,1:T(8,128)(2,1)S(1)}, u32[]{:S(2)}, u32[]{:S(2)}) async-start(bf16[128,32,128]{2,0,1:T(8,128)(2,1)} %copy.122), calls=%async_computation.3 | async-start | bytes 2097152 | tf_op jit(solution)/shard_map/all_to_all | solution.py:15
  42.0 119.8 %all-gather.6.cloned.1.call-start = ((), (), s32[]{:S(2)}) async-start(), calls=%async_computation.9 | async-start | bytes 4325376 | tf_op jit(solution)/shard_map/all_gather | solution.py:49
  43.9 123.8 %copy-start.8 = (f32[1024,4]{0,1:T(4,128)}, f32[1024,4]{0,1:T(4,128)S(1)}, u32[]{:S(2)}) copy-start(f32[1024,4]{0,1:T(4,128)S(1)} %get-tuple-element.7) | copy-start | bytes 49156
  44.0 18.7 %copy-start.1 = (bf16[128,8,4,128]{3,0,1,2:T(8,128)(2,1)}, bf16[128,8,4,128]{3,0,1,2:T(8,128)(2,1)S(1)}, u32[]{:S(2)}) copy-start(bf16[128,8,4,128]{3,0,1,2:T(8,128)(2,1)S(1)} %copy.121) | copy-start | bytes 3145732
  57.1 1.0 copy-start.4
  57.1 10.0 %copy-start.7 = (bf16[128,32,128]{2,1,0:T(8,128)(2,1)S(1)}, bf16[128,32,128]{2,1,0:T(8,128)(2,1)}, u32[]{:S(2)}) copy-start(bf16[128,32,128]{2,1,0:T(8,128)(2,1)} %param.8) | copy-start | bytes 3145732
  62.7 19.4 %all-to-all-start = ((bf16[128,32,128]{2,0,1:T(8,128)(2,1)}), bf16[128,32,128]{2,0,1:T(8,128)(2,1)S(1)}, u32[]{:S(2)}, u32[]{:S(2)}) async-start(bf16[128,32,128]{2,0,1:T(8,128)(2,1)} %copy.118), calls=%async_computation | async-start | bytes 2097152 | tf_op jit(solution)/shard_map/all_to_all | solution.py:13
  82.1 19.4 %all-to-all-start.5 = ((bf16[128,32,128]{2,0,1:T(8,128)(2,1)}), bf16[128,32,128]{2,0,1:T(8,128)(2,1)S(1)}, u32[]{:S(2)}, u32[]{:S(2)}) async-start(bf16[128,32,128]{2,0,1:T(8,128)(2,1)} %copy.132), calls=%async_computation.5 | async-start | bytes 2097152 | tf_op jit(solution)/shard_map/all_to_all | solution.py:16
  86.5 134.6 %all-gather.8.cloned.1.call-start = ((), (), s32[]{:S(2)}) async-start(), calls=%async_computation.10 | async-start | bytes 4325376 | tf_op jit(solution)/shard_map/all_gather | solution.py:55
  142.7 7.4 %copy-start.2 = (bf16[128,8,4,128]{3,0,1,2:T(8,128)(2,1)S(1)}, bf16[128,8,4,128]{3,0,1,2:T(8,128)(2,1)}, u32[]{:S(2)}) copy-start(bf16[128,8,4,128]{3,0,1,2:T(8,128)(2,1)} %copy-done.1) | copy-start | bytes 3145732
  150.0 4.0 %copy-start = (bf16[4,1024,1024]{2,1,0:T(8,128)(2,1)}, bf16[4,1024,1024]{2,1,0:T(8,128)(2,1)S(1)}, u32[]{:S(2)}) copy-start(bf16[4,1024,1024]{2,1,0:T(8,128)(2,1)S(1)} %multiply_convert_fusion) | copy-start | bytes 25165828
  161.8 5.9 %copy-start.5 = (f32[4,1024,128]{2,1,0:T(8,128)S(1)}, f32[4,1024,128]{2,1,0:T(8,128)}, u32[]{:S(2)}) copy-start(f32[4,1024,128]{2,1,0:T(8,128)} %fusion.14) | copy-start | bytes 6291460
  170.4 59.9 %all-to-all-start.6 = ((bf16[1024,4,128]{2,1,0:T(4,128)(2,1)}), bf16[1024,4,128]{2,1,0:T(4,128)(2,1)S(1)}, u32[]{:S(2)}, u32[]{:S(2)}) async-start(bf16[1024,4,128]{2,1,0:T(4,128)(2,1)} %copy.135), calls=%async_computation.6 | async-start | bytes 2097152 | tf_op jit(solution)/shard_map/all_to_all | solution.py:92
  230.3 23.5 %all-to-all-start.7 = ((bf16[1024,4,128]{2,1,0:T(4,128)(2,1)}), bf16[1024,4,128]{2,1,0:T(4,128)(2,1)}, u32[]{:S(2)}, u32[]{:S(2)}) async-start(bf16[1024,4,128]{2,1,0:T(4,128)(2,1)} %copy.141), calls=%async_computation.7 | async-start | bytes 2097152 | tf_op jit(solution)/shard_map/all_to_all | solution.py:93
  238.8 6.0 %copy-start.9 = (f32[1024,4]{0,1:T(4,128)S(1)}, f32[1024,4]{0,1:T(4,128)}, u32[]{:S(2)}) copy-start(f32[1024,4]{0,1:T(4,128)} %copy-done.8) | copy-start | bytes 49156
  253.8 19.4 %all-to-all-start.4 = ((bf16[1024,4,128]{2,1,0:T(4,128)(2,1)}), bf16[1024,4,128]{2,1,0:T(4,128)(2,1)S(1)}, u32[]{:S(2)}, u32[]{:S(2)}) async-start(bf16[1024,4,128]{2,1,0:T(4,128)(2,1)} %copy.130), calls=%async_computation.4 | async-start | bytes 2097152 | tf_op jit(solution)/shard_map/all_to_all | solution.py:91
  258.3 6.4 %copy-start.3 = (bf16[128,8,4,128]{3,0,1,2:T(8,128)(2,1)S(1)}, bf16[128,8,4,128]{3,0,1,2:T(8,128)(2,1)}, u32[]{:S(2)}) copy-start(bf16[128,8,4,128]{3,0,1,2:T(8,128)(2,1)} %copy-done.1) | copy-start | bytes 3145732
  273.3 19.4 %all-to-all-start.8 = ((bf16[1024,4,128]{2,1,0:T(4,128)(2,1)}), bf16[1024,4,128]{2,1,0:T(4,128)(2,1)S(1)}, u32[]{:S(2)}, u32[]{:S(2)}) async-start(bf16[1024,4,128]{2,1,0:T(4,128)(2,1)} %copy.145), calls=%async_computation.8 | async-start | bytes 2097152 | tf_op jit(solution)/shard_map/all_to_all | solution.py:94
Sparse Core Ops, SparseCore 0:
  60.2 79.0 all-gather.5
  142.4 78.6 all-gather.7
where the time goes:
time: 302 us; the launch traced here: 301 us
  waiting for transfers between devices  114 us (38%)
  matrix products  54.6 us (18%)
  starting transfers between devices  49.5 us (16%)
  blocking collectives  38.2 us (13%)
  local copies, waits for them, and re-layouts  24.7 us (8%)
  between operations  14.3 us (5%)
  other arithmetic  5.77 us (2%)
    all_gather x1, blocking collectives, shards(): totals = lax.all_gather(seg_total[None, :], 'seq', axis=0, tiled=True)  38.2 us
    all_gather x1, waiting for transfers between devices, shards(): lax.all_gather(local_qg[None], 'seq', axis=0, tiled=True).astype(f32)  34.8 us
    all_to_all x1, waiting for transfers between devices, shards(): lax.all_to_all(grad_out, 'head', split_axis=1, concat_axis=0, tiled=True)  14.9 us
    all_to_all x1, waiting for transfers between devices, shards(): lax.all_to_all(key_in, 'head', split_axis=1, concat_axis=0, tiled=True)  13.6 us
    all_to_all x1, waiting for transfers between devices, shards(): lax.all_to_all(query_in, 'head', split_axis=1, concat_axis=0, tiled=True)  13.6 us
    all_to_all x1, waiting for transfers between devices, shards(): lax.all_to_all(value_in, 'head', split_axis=1, concat_axis=0, tiled=True)  13 us
    all_to_all x1, waiting for transfers between devices, shards(): lax.all_to_all(grad_value, 'head', split_axis=0, concat_axis=1, tiled=True)  9.78 us
    unnamed x27, local copies, waits for them, and re-layouts  9.06 us
  transfers between devices with their start and end apart: 11, of which 9 were waited for; matrix products, arithmetic and copies ran while one was open for 27% of the time, Pallas kernels for 0%

commit v1 on v0

v1 whole, which is shorter than its diff:
```python
import functools

import jax
import jax.numpy as jnp
from jax import lax
from jax.experimental import pallas as pl
from jax.experimental.pallas import tpu as pltpu
from jax.sharding import PartitionSpec as P

precise = lax.Precision.HIGHEST
f32 = jnp.float32
bf16 = jnp.bfloat16


def columns(row, width):
    return jnp.transpose(jnp.broadcast_to(row, (width, row.shape[1])))


def local_states_kernel(q_ref, k_ref, v_ref, g_ref, within_ref, kv_ref, qg_ref):
    width = q_ref.shape[-1]
    length = within_ref.shape[-1]
    col = columns(within_ref[...], width)
    total = col[length - 1 :, :]
    k_end = (k_ref[...].reshape(length, width).astype(f32) * jnp.exp(total - col)).astype(bf16)
    q_start = (q_ref[...].reshape(length, width).astype(f32) * jnp.exp(col)).astype(bf16)
    over_rows = (((0,), (0,)), ((), ()))
    kv_ref[...] = lax.dot_general(
        k_end, v_ref[...].reshape(length, width), over_rows, preferred_element_type=f32
    ).astype(bf16)
    qg_ref[...] = lax.dot_general(
        q_start, g_ref[...].reshape(length, width), over_rows, preferred_element_type=f32
    ).astype(bf16)


def attention_kernel(swap, tile, q_ref, k_ref, v_ref, g_ref, within_ref, in_ref, out_ref, o_ref):
    width = q_ref.shape[-1]
    length = within_ref.shape[-1]
    pieces = q_ref.shape[0]
    scaling = 1.0 / width
    row = within_ref[...]
    col = columns(row, width)
    total = col[length - 1 :, :]
    q = q_ref[...].reshape(length, width)
    k = k_ref[...].reshape(length, width)
    v = v_ref[...].reshape(length, width)
    g = g_ref[...].reshape(length, width)
    count = length // tile
    cut = lambda x, i: x[i * tile : (i + 1) * tile, :]
    state_dims = (((1,), (1 if swap else 0,)), ((), ()))
    by_key = [None] * count
    per = pieces // count
    for i in range(count):
        q_i, g_i, col_i = cut(q, i), cut(g, i), cut(col, i)
        wide = jnp.concatenate([col_i] * (tile // width), axis=1)
        q_start = (q_i.astype(f32) * jnp.exp(col_i)).astype(bf16)
        acc = scaling * lax.dot_general(q_start, in_ref[...], state_dims, preferred_element_type=f32)
        for j in range(i + 1):
            s = lax.dot_general(q_i, cut(k, j), (((1,), (1,)), ((), ())), preferred_element_type=f32)
            gap = wide - row[:, j * tile : (j + 1) * tile]
            if i == j:
                keep = lax.broadcasted_iota(jnp.int32, (tile, tile), 0) >= lax.broadcasted_iota(
                    jnp.int32, (tile, tile), 1
                )
                decay = jnp.where(keep, jnp.exp(jnp.where(keep, gap, 0.0)), 0.0)
            else:
                decay = jnp.exp(gap)
            w = (scaling * s * decay).astype(bf16)
            acc = acc + lax.dot_general(w, cut(v, j), (((1,), (0,)), ((), ())), preferred_element_type=f32)
            back = lax.dot_general(w, g_i, (((0,), (0,)), ((), ())), preferred_element_type=f32)
            by_key[j] = back if by_key[j] is None else by_key[j] + back
        o_ref[i * per : (i + 1) * per, 0] = acc.astype(bf16).reshape(per, -1, width)
    for j in range(count):
        k_end = (cut(k, j).astype(f32) * jnp.exp(total - cut(col, j))).astype(bf16)
        acc = by_key[j] + scaling * lax.dot_general(
            k_end, out_ref[...], state_dims, preferred_element_type=f32
        )
        o_ref[j * per : (j + 1) * per, 1] = acc.astype(bf16).reshape(per, -1, width)


def shards(query_in, key_in, value_in, grad_out, log_decay):
    tokens, all_heads, width = query_in.shape
    groups = lax.axis_size("head")
    heads = all_heads // groups
    segs = lax.axis_size("seq")
    length = tokens * groups

    def scatter_heads(a, b):
        pair = jnp.stack([a, b]).reshape(2, tokens, groups, heads, width).transpose(2, 0, 3, 1, 4)
        return lax.all_to_all(pair, "head", split_axis=0, concat_axis=0, tiled=True)

    decays = log_decay.reshape(tokens, groups, heads).transpose(1, 2, 0)
    decays = lax.all_to_all(decays, "head", split_axis=0, concat_axis=0, tiled=True)
    within = jnp.cumsum(decays.astype(f32).transpose(1, 0, 2).reshape(heads, length), axis=1)
    totals = lax.all_to_all(
        jnp.broadcast_to(within[None, :, -1], (segs, heads)), "seq", split_axis=0, concat_axis=0, tiled=True
    )
    within = within[:, None, :]
    kv_in = scatter_heads(key_in, value_in)
    qg_in = scatter_heads(query_in, grad_out)

    cum_inc = jnp.cumsum(totals, axis=0)
    cum_exc = cum_inc - totals
    ranks = jnp.arange(segs)
    earlier = (ranks[None, :] < ranks[:, None])[:, :, None]
    later_on = (ranks[None, :] > ranks[:, None])[:, :, None]
    w_in = jnp.where(
        earlier, jnp.exp(jnp.where(earlier, cum_exc[:, None, :] - cum_inc[None, :, :], 0.0)), 0.0
    )
    w_out = jnp.where(
        later_on, jnp.exp(jnp.where(later_on, cum_exc[None, :, :] - cum_inc[:, None, :], 0.0)), 0.0
    )
    weights = jnp.stack([w_in, w_out]).transpose(0, 3, 1, 2)

    def part(which):
        return pl.BlockSpec((groups, None, None, tokens, width), lambda h: (0, which, h, 0, 0))

    row = pl.BlockSpec((None, 1, length), lambda h: (h, 0, 0))
    square = pl.BlockSpec((None, width, width), lambda h: (h, 0, 0))
    state = jax.ShapeDtypeStruct((heads, width, width), bf16)
    local_kv, local_qg = pl.pallas_call(
        local_states_kernel,
        grid=(heads,),
        in_specs=[part(0), part(0), part(1), part(1), row],
        out_specs=[square, square],
        out_shape=[state, state],
    )(qg_in, kv_in, kv_in, qg_in, within)

    rows = width // segs
    local = jnp.stack([local_kv, local_qg]).reshape(2, heads, segs, rows * width).transpose(2, 0, 1, 3)
    gathered = lax.all_to_all(local, "seq", split_axis=0, concat_axis=0, tiled=True)
    states = jnp.einsum("chji,ichr->jchr", weights, gathered.astype(f32), precision=precise).astype(bf16)
    states = lax.all_to_all(states, "seq", split_axis=0, concat_axis=0, tiled=True)
    states = states.transpose(1, 2, 0, 3).reshape(2, heads, width, width)

    def attention(swap, q, k, v, g):
        return pl.pallas_call(
            functools.partial(attention_kernel, swap, min(256, length)),
            grid=(heads,),
            in_specs=[
                part(q[1]), part(k[1]), part(v[1]), part(g[1]), row,
                pl.BlockSpec((None, None, width, width), lambda h: (0, h, 0, 0)),
                pl.BlockSpec((None, None, width, width), lambda h: (1, h, 0, 0)),
            ],
            out_specs=pl.BlockSpec((groups, 2, None, tokens, width), lambda h: (0, 0, h, 0, 0)),
            out_shape=jax.ShapeDtypeStruct((groups, 2, heads, tokens, width), bf16),
            cost_estimate=pl.CostEstimate(
                flops=6 * heads * length * length * width,
                bytes_accessed=12 * heads * length * width,
                transcendentals=heads * length * length // 2,
            ),
        )(q[0], k[0], v[0], g[0], within, states, states)

    queries, grads, keys, values = (qg_in, 0), (qg_in, 1), (kv_in, 0), (kv_in, 1)
    first = attention(False, queries, keys, values, grads)
    second = attention(True, grads, values, keys, queries)

    def gather_heads(pair):
        pair = lax.all_to_all(pair, "head", split_axis=0, concat_axis=0, tiled=True)
        pair = pair.transpose(1, 3, 0, 2, 4).reshape(2, tokens, all_heads, width)
        return pair[0], pair[1]

    attended, grad_value = gather_heads(first)
    grad_query, grad_key = gather_heads(second)
    return attended, grad_query, grad_key, grad_value


def solution(mesh):
    tall = P(("seq", "head"), None, None)
    return jax.shard_map(
        shards,
        mesh=mesh,
        in_specs=(tall, tall, tall, tall, P(("seq", "head"), None)),
        out_specs=(tall, tall, tall, tall),
        check_vma=False,
    )
```

time: 302 us -> 212 us (0.70)
  matrix products: 54.6 us -> 0.41 us
  Pallas kernels: 0 us -> 29.6 us
  blocking collectives: 38.2 us -> 15.1 us
  waiting for transfers between devices: 114 us -> 95.9 us
  between operations: 14.3 us -> 0.8 us
  local copies, waits for them, and re-layouts: 24.7 us -> 16.8 us
    dot_general x13 -> x1, matrix products: 54.6 us -> 0.41 us  [shards(): jnp.einsum('chji,ichr->jchr', weights, gathered.astype(f32), precision=pr...]
    all_gather x1 -> x0, blocking collectives: 38.2 us -> none  [shards(): totals = lax.all_gather(seg_total[None, :], 'seq', axis=0, tiled=True)]
    all_gather x2 -> x0, waiting for transfers between devices: 34.8 us -> none  [the longest x1 34.8 us: shards(): lax.all_gather(local_qg[None], 'seq', axis=0, tiled=True).astype(f32)]
    pallas_call x0 -> x3, Pallas kernels: none -> 29.6 us  [the longest x2 24.8 us: attention(): pl.pallas_call(functools.partial(attention_kernel, swap, min(256, length)...]
    all_to_all x9 -> x7, waiting for transfers between devices: 79.1 us -> 95.9 us  [the longest x2 47.6 us: scatter_heads(): return lax.all_to_all(pair, 'head', split_axis=0, concat_axis=0, tiled=True)]
    all_to_all x0 -> x1, blocking collectives: none -> 15.1 us  [shards(): lax.all_to_all(states, 'seq', split_axis=0, concat_axis=0, tiled=True)]
    convert_element_type x4 -> x1, local copies, waits for them, and re-layouts: 7.13 us -> 0.21 us  [shards(): jnp.einsum('chji,ichr->jchr', weights, gathered.astype(f32), precision=pr...]
    all_to_all x8 -> x2, local copies, waits for them, and re-layouts: 6.94 us -> 0.17 us  [shards(): lax.all_to_all(jnp.broadcast_to(within[None, :, -1], (segs, heads)), 'seq...]
  transfers between devices with their start and end apart: 11 -> 7, of which waited for: 9 -> 7; matrix products, arithmetic and copies ran while one was open for 27% -> 7% of each run, Pallas kernels for 0% -> 8%
where the time goes in v1:
time: 212 us
  waiting for transfers between devices  95.9 us (45%)
  starting transfers between devices  47.5 us (22%)
  Pallas kernels  29.6 us (14%)
  local copies, waits for them, and re-layouts  16.8 us (8%)
  blocking collectives  15.1 us (7%)
  other arithmetic  5.5 us (3%)
    all_to_all x2, waiting for transfers between devices, scatter_heads(): return lax.all_to_all(pair, 'head', split_axis=0, concat_axis=0, tiled=True)  47.6 us
    all_to_all x2, waiting for transfers between devices, gather_heads(): pair = lax.all_to_all(pair, 'head', split_axis=0, concat_axis=0, tiled=True)  36.7 us
    pallas_call x2, Pallas kernels, attention(): pl.pallas_call(functools.partial(attention_kernel, swap, min(256, length)...  24.8 us
    all_to_all x1, blocking collectives, shards(): lax.all_to_all(states, 'seq', split_axis=0, concat_axis=0, tiled=True)  15.1 us
    all_to_all x2, starting transfers between devices, gather_heads(): pair = lax.all_to_all(pair, 'head', split_axis=0, concat_axis=0, tiled=True)  12.5 us
    all_to_all x1, starting transfers between devices, shards(): lax.all_to_all(jnp.broadcast_to(within[None, :, -1], (segs, heads)), 'seq...  10.5 us
    unnamed x18, local copies, waits for them, and re-layouts  10.3 us
    all_to_all x1, waiting for transfers between devices, shards(): lax.all_to_all(local, 'seq', split_axis=0, concat_axis=0, tiled=True)  9.87 us
  transfers between devices with their start and end apart: 7, of which 7 were waited for; matrix products, arithmetic and copies ran while one was open for 7% of the time, Pallas kernels for 8%

profile of v1, /device:TPU:1, one launch (start us, length us, event | category | flops | bytes accessed | tf_op | source)
XLA Modules:
  0.0 211.6 jit_solution(16733741976977138399)
XLA Ops:
  0.6 6.6 %all-to-all-start.2 = ((bf16[8,4,128]{2,1,0:T(4,128)(2,1)}), bf16[8,4,128]{2,1,0:T(4,128)(2,1)S(1)}, u32[]{:S(2)}, u32[]{:S(2)}) async-start(bf16[8,4,128]{2,1,0:T(4,128)(2,1)} %bitcast.57), calls=%async_computation.2 | async-start | bytes 16384 | tf_op jit(solution)/shard_map/all_to_all | solution.py:92
  7.2 1.6 copy.43
  9.3 1.5 maximum_bitcast_fusion.1
  10.8 1.1 all-to-all-done.2
  11.9 4.2 %all-to-all-start.1 = ((bf16[8,2,4,128,128]{4,3,2,1,0:T(8,128)(2,1)}), bf16[8,2,4,128,128]{4,3,2,1,0:T(8,128)(2,1)S(1)}, u32[]{:S(2)}, u32[]{:S(2)}) async-start(bf16[8,2,4,128,128]{4,3,2,1,0:T(8,128)(2,1)} %maximum_bitcast_fusion.1), calls=%async_computation.1 | async-start | bytes 4194304 | tf_op jit(solution)/shard_map/all_to_all | solution.py:89
  16.5 0.8 copy-done.3
  17.7 1.5 maximum_bitcast_fusion
  19.2 23.1 %all-to-all-done.1.k_ref.v_ref = bf16[8,2,4,128,128]{4,3,2,1,0:T(8,128)(2,1)S(1)} async-done(((bf16[8,2,4,128,128]{4,3,2,1,0:T(8,128)(2,1)}), bf16[8,2,4,128,128]{4,3,2,1,0:T(8,128)(2,1)S(1)}, u32[]{:S(2)}, u32[]{:S(2)}) %all-to-all-start.1) | async-done | bytes 2097184 | tf_op jit(solution)/shard_map/all_to_all | solution.py:89
  42.3 5.2 %all-to-all-start = ((bf16[8,2,4,128,128]{4,3,2,1,0:T(8,128)(2,1)}), bf16[8,2,4,128,128]{4,3,2,1,0:T(8,128)(2,1)}, u32[]{:S(2)}, u32[]{:S(2)}) async-start(bf16[8,2,4,128,128]{4,3,2,1,0:T(8,128)(2,1)} %maximum_bitcast_fusion), calls=%async_computation | async-start | bytes 4194304 | tf_op jit(solution)/shard_map/all_to_all | solution.py:89
  47.5 1.1 reduce-window.6
  49.3 24.5 %all-to-all-done.q_ref.g_ref = bf16[8,2,4,128,128]{4,3,2,1,0:T(8,128)(2,1)} async-done(((bf16[8,2,4,128,128]{4,3,2,1,0:T(8,128)(2,1)}), bf16[8,2,4,128,128]{4,3,2,1,0:T(8,128)(2,1)}, u32[]{:S(2)}, u32[]{:S(2)}) %all-to-all-start) | async-done | bytes 2097184 | tf_op jit(solution)/shard_map/all_to_all | solution.py:89
  74.4 10.5 %all-to-all-start.4 = ((f32[32,1,4]{2,1,0:T(1,128)}), f32[32,1,4]{2,1,0:T(1,128)S(1)}, u32[]{:S(2)}, u32[]{:S(2)}) async-start(f32[32,1,4]{2,1,0:T(1,128)} %broadcast_in_dim.50), calls=%async_computation.4 | async-start | bytes 32768 | tf_op jit(solution)/shard_map/all_to_all | solution.py:94
  85.0 4.8 %shard_map.84 = (bf16[4,128,128]{2,1,0:T(8,128)(2,1)}, bf16[4,128,128]{2,1,0:T(8,128)(2,1)}) custom-call(bf16[8,2,4,128,128]{4,3,2,1,0:T(8,128)(2,1)} %all-to-all-done.q_ref.g_ref, bf16[8,2,4,128,128]{4,3,2,1,0:T(8,128)(2,1)} %copy-done, bf16[8,2,4,128,128]{4,3,2,1,0:T(8,128)(2,1)} %copy-done, bf16[8,2,4,128,128]{4,3,2,1,0:T(8,128)(2,1)} %all-to-all-done.q_ref.g_ref, ...), custom_call_target="tpu_custom_call" | custom-call | tf_op jit(solution)/shard_map/pallas_call | solution.py:120
  89.8 1.0 stack.38
  90.9 1.0 stack.39
  92.0 0.9 maximum_bitcast_fusion.2
  92.9 0.7 all-to-all-done.4
  93.5 8.5 %all-to-all-start.3 = ((bf16[32,2,4,512]{3,2,1,0:T(4,128)(2,1)}), bf16[32,2,4,512]{3,2,1,0:T(4,128)(2,1)S(1)}, u32[]{:S(2)}, u32[]{:S(2)}) async-start(bf16[32,2,4,512]{3,2,1,0:T(4,128)(2,1)} %maximum_bitcast_fusion.2), calls=%async_computation.3 | async-start | bytes 524288 | tf_op jit(solution)/shard_map/all_to_all | solution.py:130
  102.6 9.9 %all-to-all-done.3 = bf16[32,2,4,512]{3,2,1,0:T(4,128)(2,1)S(1)} async-done(((bf16[32,2,4,512]{3,2,1,0:T(4,128)(2,1)}), bf16[32,2,4,512]{3,2,1,0:T(4,128)(2,1)S(1)}, u32[]{:S(2)}, u32[]{:S(2)}) %all-to-all-start.3) | async-done | bytes 262176 | tf_op jit(solution)/shard_map/all_to_all | solution.py:130
  113.1 15.1 %all_to_all.44 = bf16[32,2,4,512]{3,2,1,0:T(4,128)(2,1)S(1)} all-to-all(bf16[32,2,4,512]{3,2,1,0:T(4,128)(2,1)S(1)} %copy.58), channel_id=1, replica_groups=mesh['seq'=32,'head'=8] {'seq'}, dimensions={0} | all-to-all | bytes 524288 | tf_op jit(solution)/shard_map/all_to_all | solution.py:132
  128.3 0.9 reshape.138.in_ref.out_ref
  129.2 12.4 %shard_map.85 = bf16[8,2,4,128,128]{4,3,2,1,0:T(8,128)(2,1)} custom-call(bf16[8,2,4,128,128]{4,3,2,1,0:T(8,128)(2,1)} %all-to-all-done.q_ref.g_ref, bf16[8,2,4,128,128]{4,3,2,1,0:T(8,128)(2,1)} %copy-done, bf16[8,2,4,128,128]{4,3,2,1,0:T(8,128)(2,1)} %copy-done, bf16[8,2,4,128,128]{4,3,2,1,0:T(8,128)(2,1)} %all-to-all-done.q_ref.g_ref, ...), custom_call_target="tpu_custom_call" | custom-call | flops 3221225472 | bytes 6291456 | tf_op jit(solution)/shard_map/pallas_call | solution.py:136
  141.6 7.3 %all-to-all-start.6 = ((bf16[8,2,4,128,128]{4,3,2,1,0:T(8,128)(2,1)}), bf16[8,2,4,128,128]{4,3,2,1,0:T(8,128)(2,1)S(1)}, u32[]{:S(2)}, u32[]{:S(2)}) async-start(bf16[8,2,4,128,128]{4,3,2,1,0:T(8,128)(2,1)} %shard_map.85), calls=%async_computation.6 | async-start | bytes 4194304 | tf_op jit(solution)/shard_map/all_to_all | solution.py:158
  148.8 12.4 %shard_map.86 = bf16[8,2,4,128,128]{4,3,2,1,0:T(8,128)(2,1)} custom-call(bf16[8,2,4,128,128]{4,3,2,1,0:T(8,128)(2,1)} %all-to-all-done.q_ref.g_ref, bf16[8,2,4,128,128]{4,3,2,1,0:T(8,128)(2,1)} %copy-done, bf16[8,2,4,128,128]{4,3,2,1,0:T(8,128)(2,1)} %copy-done, bf16[8,2,4,128,128]{4,3,2,1,0:T(8,128)(2,1)} %all-to-all-done.q_ref.g_ref, ...), custom_call_target="tpu_custom_call" | custom-call | flops 3221225472 | bytes 6291456 | tf_op jit(solution)/shard_map/pallas_call | solution.py:136
  161.2 13.8 %all-to-all-done.6 = bf16[8,2,4,128,128]{4,3,2,1,0:T(8,128)(2,1)S(1)} async-done(((bf16[8,2,4,128,128]{4,3,2,1,0:T(8,128)(2,1)}), bf16[8,2,4,128,128]{4,3,2,1,0:T(8,128)(2,1)S(1)}, u32[]{:S(2)}, u32[]{:S(2)}) %all-to-all-start.6) | async-done | bytes 2097184 | tf_op jit(solution)/shard_map/all_to_all | solution.py:158
  175.1 5.2 %all-to-all-start.7 = ((bf16[8,2,4,128,128]{4,3,2,1,0:T(8,128)(2,1)}), bf16[8,2,4,128,128]{4,3,2,1,0:T(8,128)(2,1)}, u32[]{:S(2)}, u32[]{:S(2)}) async-start(bf16[8,2,4,128,128]{4,3,2,1,0:T(8,128)(2,1)} %shard_map.86), calls=%async_computation.7 | async-start | bytes 4194304 | tf_op jit(solution)/shard_map/all_to_all | solution.py:158
  180.4 1.6 copy.63
  182.0 1.6 copy.60
  183.7 22.9 %all-to-all-done.7 = bf16[8,2,4,128,128]{4,3,2,1,0:T(8,128)(2,1)} async-done(((bf16[8,2,4,128,128]{4,3,2,1,0:T(8,128)(2,1)}), bf16[8,2,4,128,128]{4,3,2,1,0:T(8,128)(2,1)}, u32[]{:S(2)}, u32[]{:S(2)}) %all-to-all-start.7) | async-done | bytes 2097184 | tf_op jit(solution)/shard_map/all_to_all | solution.py:158
  206.6 1.7 fusion.7
  208.3 1.6 copy.62
  209.9 1.6 copy.61
  (35 shorter events, 4.1 us)
Async XLA Ops:
  0.6 8.2 %copy-start.1 = (bf16[128,32,128]{2,1,0:T(8,128)(2,1)S(1)}, bf16[128,32,128]{2,1,0:T(8,128)(2,1)}, u32[]{:S(2)}) copy-start(bf16[128,32,128]{2,1,0:T(8,128)(2,1)} %param.7) | copy-start | bytes 3145732
  0.6 11.2 %all-to-all-start.2 = ((bf16[8,4,128]{2,1,0:T(4,128)(2,1)}), bf16[8,4,128]{2,1,0:T(4,128)(2,1)S(1)}, u32[]{:S(2)}, u32[]{:S(2)}) async-start(bf16[8,4,128]{2,1,0:T(4,128)(2,1)} %bitcast.57), calls=%async_computation.2 | async-start | bytes 16384 | tf_op jit(solution)/shard_map/all_to_all | solution.py:92
  10.8 5.3 %copy-start.2 = (bf16[128,32,128]{2,1,0:T(8,128)(2,1)S(1)}, bf16[128,32,128]{2,1,0:T(8,128)(2,1)}, u32[]{:S(2)}) copy-start(bf16[128,32,128]{2,1,0:T(8,128)(2,1)} %param.5) | copy-start | bytes 3145732
  11.9 30.4 %all-to-all-start.1 = ((bf16[8,2,4,128,128]{4,3,2,1,0:T(8,128)(2,1)}), bf16[8,2,4,128,128]{4,3,2,1,0:T(8,128)(2,1)S(1)}, u32[]{:S(2)}, u32[]{:S(2)}) async-start(bf16[8,2,4,128,128]{4,3,2,1,0:T(8,128)(2,1)} %maximum_bitcast_fusion.1), calls=%async_computation.1 | async-start | bytes 4194304 | tf_op jit(solution)/shard_map/all_to_all | solution.py:89
  16.1 1.2 copy-start.3
  42.3 5.2 %copy-start = (bf16[8,2,4,128,128]{4,3,2,1,0:T(8,128)(2,1)}, bf16[8,2,4,128,128]{4,3,2,1,0:T(8,128)(2,1)S(1)}, u32[]{:S(2)}) copy-start(bf16[8,2,4,128,128]{4,3,2,1,0:T(8,128)(2,1)S(1)} %all-to-all-done.1.k_ref.v_ref) | copy-start | bytes 6291460
  42.3 31.5 %all-to-all-start = ((bf16[8,2,4,128,128]{4,3,2,1,0:T(8,128)(2,1)}), bf16[8,2,4,128,128]{4,3,2,1,0:T(8,128)(2,1)}, u32[]{:S(2)}, u32[]{:S(2)}) async-start(bf16[8,2,4,128,128]{4,3,2,1,0:T(8,128)(2,1)} %maximum_bitcast_fusion), calls=%async_computation | async-start | bytes 4194304 | tf_op jit(solution)/shard_map/all_to_all | solution.py:89
  49.1 35.9 %copy-start.4 = (f32[4,8,128]{2,1,0:T(8,128)}, f32[4,8,128]{2,1,0:T(8,128)S(1)}, u32[]{:S(2)}) copy-start(f32[4,8,128]{2,1,0:T(8,128)S(1)} %broadcast_add_fusion) | copy-start | bytes 49156
  74.4 19.1 %all-to-all-start.4 = ((f32[32,1,4]{2,1,0:T(1,128)}), f32[32,1,4]{2,1,0:T(1,128)S(1)}, u32[]{:S(2)}, u32[]{:S(2)}) async-start(f32[32,1,4]{2,1,0:T(1,128)} %broadcast_in_dim.50), calls=%async_computation.4 | async-start | bytes 32768 | tf_op jit(solution)/shard_map/all_to_all | solution.py:94
  93.5 19.0 %all-to-all-start.3 = ((bf16[32,2,4,512]{3,2,1,0:T(4,128)(2,1)}), bf16[32,2,4,512]{3,2,1,0:T(4,128)(2,1)S(1)}, u32[]{:S(2)}, u32[]{:S(2)}) async-start(bf16[32,2,4,512]{3,2,1,0:T(4,128)(2,1)} %maximum_bitcast_fusion.2), calls=%async_computation.3 | async-start | bytes 524288 | tf_op jit(solution)/shard_map/all_to_all | solution.py:130
  141.6 33.5 %all-to-all-start.6 = ((bf16[8,2,4,128,128]{4,3,2,1,0:T(8,128)(2,1)}), bf16[8,2,4,128,128]{4,3,2,1,0:T(8,128)(2,1)S(1)}, u32[]{:S(2)}, u32[]{:S(2)}) async-start(bf16[8,2,4,128,128]{4,3,2,1,0:T(8,128)(2,1)} %shard_map.85), calls=%async_computation.6 | async-start | bytes 4194304 | tf_op jit(solution)/shard_map/all_to_all | solution.py:158
  175.1 31.5 %all-to-all-start.7 = ((bf16[8,2,4,128,128]{4,3,2,1,0:T(8,128)(2,1)}), bf16[8,2,4,128,128]{4,3,2,1,0:T(8,128)(2,1)}, u32[]{:S(2)}, u32[]{:S(2)}) async-start(bf16[8,2,4,128,128]{4,3,2,1,0:T(8,128)(2,1)} %shard_map.86), calls=%async_computation.7 | async-start | bytes 4194304 | tf_op jit(solution)/shard_map/all_to_all | solution.py:158
